TPU v7x, 32 devices: a whole 2x2x4 slice. The times are simulated.
32 devices in a mesh: grp: 4 (over z), mem: 8 (over y, x, core).
Axes of the slice: x: 2, y: 2, z: 4, core: 2. Of those that a mesh axis runs over, the one named last changes fastest.
Arguments:
- basis: float32 [20, 2048, 128], P(None, ('grp', 'mem'))
- precond: bfloat16 [2048, 128, 128], P(('grp', 'mem'))
- leaf_rows: float32 [1024, 128], P(('grp', 'mem')), may hold values from -6 to 6
- leaf_fiber: int32 [1024], P(('grp', 'mem')), may hold values from 0 to 63
- strad_rows: float32 [1024, 128], P(('grp', 'mem')), may hold values from -6 to 6
- strad_fiber: int32 [1024], P(('grp', 'mem')), may hold values from 0 to 63
- strad_count: int32 [32, 4], P(('grp', 'mem')), may hold values from 0 to 8, as said below
Outputs:
- coeffs: float32 [21], replicated
- next_vector: float32 [2048, 128], P(('grp', 'mem'))
Inputs may be any that keep to these rules, and one draw needn't show every extreme that they name: `leaf_fiber`: a destination fiber within the destination device. `strad_fiber`: a fiber of the receiving device. The first strad_count slots of a block are live, the rest are not read; some device fills a block.
All inputs are finite; a program needn't handle non-finite values.
Results may differ from a plain program's by a relative error of at most 0.0011.
Values sent between devices are 32-bit elements; how exact they have to be, the bound alone decides.
A program may use at most 64 MiB of HBM per device.

v0:
```python
import jax
import jax.numpy as jnp
from jax import lax
from jax.sharding import PartitionSpec as P

EPS = 1e-06


def local(basis, precond, leaf_rows, leaf_fiber, strad_rows, strad_fiber, strad_count):
    groups = lax.axis_size("grp")
    members = lax.axis_size("mem")
    krylov, fibers_here, width = basis.shape
    fiber_index = jnp.arange(fibers_here, dtype=jnp.int32)
    arrived, arrived_ids = (
        lax.all_to_all(leaf_rows, "mem", split_axis=0, concat_axis=0, tiled=True),
        lax.all_to_all(
            leaf_fiber.astype(jnp.float32), "mem", split_axis=0, concat_axis=0, tiled=True
        ),
    )
    select = (fiber_index[:, None] == arrived_ids.astype(jnp.int32)[None, :]).astype(jnp.float32)
    far_field = jnp.dot(
        select, arrived, precision=lax.Precision.HIGHEST, preferred_element_type=jnp.float32
    )
    strad_slots = strad_rows.shape[0] // groups
    keeping = (jnp.arange(strad_slots, dtype=jnp.int32)[None, :] < strad_count[0][:, None]).reshape(
        -1
    )
    outgoing = strad_rows * keeping[:, None].astype(jnp.float32)
    incoming = lax.all_to_all(outgoing, "grp", split_axis=0, concat_axis=0, tiled=True)
    select_near = (fiber_index[:, None] == strad_fiber[None, :]).astype(jnp.float32)
    near_field = jnp.dot(
        select_near, incoming, precision=lax.Precision.HIGHEST, preferred_element_type=jnp.float32
    )
    field = (basis[krylov - 1] + far_field + near_field).astype(jnp.bfloat16)
    applied = jnp.einsum("fij,fj->fi", precond, field, preferred_element_type=jnp.float32)
    total = float(fibers_here * width * groups * members)
    local_coef = jnp.einsum("kfi,fi->k", basis, applied, precision=lax.Precision.HIGHEST)
    gram_local = jnp.einsum("kfi,lfi->kl", basis, basis, precision=lax.Precision.HIGHEST)
    coef_sum, square_sum, gram_sum = lax.psum(
        (local_coef, jnp.sum(applied * applied), gram_local), ("grp", "mem")
    )
    coef = coef_sum / total
    gram = gram_sum / total
    residual = applied - jnp.einsum("k,kfi->fi", coef, basis, precision=lax.Precision.HIGHEST)
    projected = jnp.dot(gram, coef, precision=lax.Precision.HIGHEST)
    square = square_sum / total - 2.0 * jnp.sum(coef * coef) + jnp.sum(coef * projected)
    beta = jnp.sqrt(square + EPS)
    return (jnp.concatenate([coef, beta[None]]), residual / beta)


def solution(mesh):
    return jax.shard_map(
        local,
        mesh=mesh,
        in_specs=(
            P(None, ("grp", "mem"), None),
            P(("grp", "mem"), None, None),
            P(("grp", "mem"), None),
            P(("grp", "mem")),
            P(("grp", "mem"), None),
            P(("grp", "mem")),
            P(("grp", "mem"), None),
        ),
        out_specs=(P(), P(("grp", "mem"), None)),
        check_vma=False,
    )
```

profile of v0, /device:TPU:0, one launch (start us, length us, event | category | flops | bytes accessed | tf_op | source)
XLA Modules:
  0.0 79.5 jit_solution(3475346898591158441)
XLA Ops:
  0.6 0.0 copy-start
  0.6 0.0 copy-start.1
  0.7 0.8 %convert_element_type.29 = f32[32]{0:T(128)S(1)} convert(s32[32]{0:T(128)} %param.10) | non-fusion elementwise | flops 32 | bytes 256 | tf_op jit(solution)/shard_map/convert_element_type | solution.py:17
  1.5 0.7 all_to_all.22
  2.1 5.2 %all-to-all-start = ((f32[8,4,1]{1,2,0:T(1,128)}), f32[8,4,1]{1,2,0:T(1,128)S(1)}, u32[]{:S(2)}, u32[]{:S(2)}) async-start(f32[8,4,1]{1,2,0:T(1,128)} %bitcast.1), calls=%async_computation | async-start | bytes 8192 | tf_op jit(solution)/shard_map/all_to_all | solution.py:16
  7.3 0.7 fusion.16
  8.1 0.1 reshape.35
  8.2 1.4 %multiply_bitcast_fusion = f32[4,8,128]{2,1,0:T(8,128)} fusion(f32[32,128]{1,0:T(8,128)} %param.11, f32[32]{0:T(128)S(1)} %reshape.35), kind=kLoop, calls=%fused_computation.21 | loop fusion | flops 4096 | bytes 32896 | tf_op jit(solution)/shard_map/all_to_all | solution.py:29
  9.5 2.8 %convolution_bitcast_fusion = f32[20,20]{1,0:T(8,128)S(1)} fusion(f32[20,64,128]{2,1,0:T(8,128)} %param.7), kind=kOutput, calls=%fused_computation.4 | convolution fusion | flops 39321600 | bytes 656960 | tf_op jit(solution)/shard_map/kfi,lfi->kl/dot_general | solution.py:38
  12.3 0.0 all-to-all-done
  12.3 4.2 %all-to-all-start.1 = ((f32[8,4,128]{2,1,0:T(4,128)}), f32[8,4,128]{2,1,0:T(4,128)S(1)}, u32[]{:S(2)}, u32[]{:S(2)}) async-start(f32[8,4,128]{2,1,0:T(4,128)} %bitcast.45), calls=%async_computation.1 | async-start | bytes 32768 | tf_op jit(solution)/shard_map/all_to_all | solution.py:15
  16.5 0.1 convert_element_type.31
  16.6 4.7 %all-to-all-done.1 = f32[8,4,128]{2,1,0:T(4,128)S(1)} async-done(((f32[8,4,128]{2,1,0:T(4,128)}), f32[8,4,128]{2,1,0:T(4,128)S(1)}, u32[]{:S(2)}, u32[]{:S(2)}) %all-to-all-start.1) | async-done | bytes 16416 | tf_op jit(solution)/shard_map/all_to_all | solution.py:15
  21.3 4.9 %all-to-all-start.2 = ((f32[4,8,128]{2,1,0:T(8,128)}), f32[4,8,128]{2,1,0:T(8,128)S(1)}, u32[]{:S(2)}, u32[]{:S(2)}) async-start(f32[4,8,128]{2,1,0:T(8,128)} %multiply_bitcast_fusion), calls=%async_computation.2 | async-start | bytes 32768 | tf_op jit(solution)/shard_map/all_to_all | solution.py:29
  26.2 0.9 %convolution_add_fusion.1 = f32[64,128]{1,0:T(8,128)S(1)} fusion(f32[32,128]{1,0:T(8,128)S(1)} %bitcast.44, f32[20,64,128]{2,1,0:T(8,128)} %param.7, s32[32]{0:T(128)S(1)} %convert_element_type.31), kind=kOutput, calls=%fused_computation.1 | convolution fusion | flops 3155968 | bytes 82048 | tf_op jit(solution)/shard_map/dot_general | solution.py:21
  27.1 4.7 %all-to-all-done.2 = f32[4,8,128]{2,1,0:T(8,128)S(1)} async-done(((f32[4,8,128]{2,1,0:T(8,128)}), f32[4,8,128]{2,1,0:T(8,128)S(1)}, u32[]{:S(2)}, u32[]{:S(2)}) %all-to-all-start.2) | async-done | bytes 16416 | tf_op jit(solution)/shard_map/all_to_all | solution.py:29
  31.8 0.8 %fusion.1 = bf16[64,128,1]{1,0,2:T(8,128)(2,1)S(1)} fusion(f32[64,128]{1,0:T(8,128)S(1)} %convolution_add_fusion.1, f32[4,8,128]{2,1,0:T(8,128)S(1)} %all-to-all-done.2, s32[32]{0:T(128)} %param.12), kind=kOutput, calls=%fused_computation.3 | convolution fusion | flops 3164160 | bytes 65664 | tf_op jit(solution)/shard_map/dot_general | solution.py:31
  32.6 0.0 copy-done
  32.6 1.2 %fusion.9 = f32[64,1,128]{2,1,0:T(1,128)S(1)} fusion(bf16[64,128,128]{2,1,0:T(8,128)(2,1)S(1)} %copy-done, bf16[64,128,1]{1,0,2:T(8,128)(2,1)S(1)} %fusion.1), kind=kOutput, calls=%fused_computation.14 | convolution fusion | flops 2097152 | bytes 2146304 | tf_op jit(solution)/shard_map/fij,fj->fi/dot_general | solution.py:35
  33.8 0.0 copy-done.1
  33.8 1.1 %convolution_bitcast_fusion.2 = f32[20]{0:T(128)S(1)} fusion(f32[20,64,128]{2,1,0:T(8,128)S(1)} %copy-done.1, f32[64,1,128]{2,1,0:T(1,128)S(1)} %fusion.9), kind=kOutput, calls=%fused_computation.7 | convolution fusion | flops 1966080 | bytes 688208 | tf_op jit(solution)/shard_map/kfi,fi->k/dot_general | solution.py:37
  34.8 0.6 multiply_reduce_fusion
  35.5 38.5 %all-reduce = (f32[]{:T(128)}, f32[20]{0:T(128)S(1)}, f32[20,20]{1,0:T(8,128)S(1)}) all-reduce(f32[]{:T(128)} %multiply_reduce_fusion, f32[20]{0:T(128)S(1)} %convolution_bitcast_fusion.2, f32[20,20]{1,0:T(8,128)S(1)} %convolution_bitcast_fusion), channel_id=1, replica_groups=mesh['grp'=4,'mem'=8] {'grp','mem'}, use_global_device_ids=true, to_apply=%region_2.0 | all-reduce | flops 421 | bytes 3368 | tf_op jit(solution)/shard_map/psum | solution.py:39
  74.0 0.6 broadcast_multiply_fusion
  74.6 0.9 %fusion.3 = f32[1,64,128]{2,0,1:T(1,128)S(1)} fusion(f32[20,64,128]{2,1,0:T(8,128)S(1)} %copy-done.1, f32[20]{0:T(128)S(1)} %get-tuple-element.3), kind=kOutput, calls=%fused_computation.8 | convolution fusion | flops 1966100 | bytes 688208 | tf_op jit(solution)/shard_map/k,kfi->fi/dot_general | solution.py:44
  75.5 0.8 %fusion.7 = f32[]{:T(128)} fusion(f32[20,20]{1,0:T(8,128)S(1)} %get-tuple-element.4, f32[20]{0:T(128)S(1)} %get-tuple-element.3), kind=kOutput, calls=%fused_computation.12 | convolution fusion | flops 5279 | bytes 1684 | tf_op jit(solution)/shard_map/dot_general | solution.py:45
  78.3 0.6 subtract_divide_fusion
  78.9 0.6 pad_maximum_fusion
  (1 shorter events, 0.0 us)
Async XLA Ops:
  0.6 31.9 %copy-start = (bf16[64,128,128]{2,1,0:T(8,128)(2,1)S(1)}, bf16[64,128,128]{2,1,0:T(8,128)(2,1)}, u32[]{:S(2)}) copy-start(bf16[64,128,128]{2,1,0:T(8,128)(2,1)} %param.8) | copy-start | bytes 6291460
  0.6 33.1 %copy-start.1 = (f32[20,64,128]{2,1,0:T(8,128)S(1)}, f32[20,64,128]{2,1,0:T(8,128)}, u32[]{:S(2)}) copy-start(f32[20,64,128]{2,1,0:T(8,128)} %param.7) | copy-start | bytes 1966084
  2.1 10.2 %all-to-all-start = ((f32[8,4,1]{1,2,0:T(1,128)}), f32[8,4,1]{1,2,0:T(1,128)S(1)}, u32[]{:S(2)}, u32[]{:S(2)}) async-start(f32[8,4,1]{1,2,0:T(1,128)} %bitcast.1), calls=%async_computation | async-start | bytes 8192 | tf_op jit(solution)/shard_map/all_to_all | solution.py:16
  12.3 9.0 %all-to-all-start.1 = ((f32[8,4,128]{2,1,0:T(4,128)}), f32[8,4,128]{2,1,0:T(4,128)S(1)}, u32[]{:S(2)}, u32[]{:S(2)}) async-start(f32[8,4,128]{2,1,0:T(4,128)} %bitcast.45), calls=%async_computation.1 | async-start | bytes 32768 | tf_op jit(solution)/shard_map/all_to_all | solution.py:15
  21.3 10.5 %all-to-all-start.2 = ((f32[4,8,128]{2,1,0:T(8,128)}), f32[4,8,128]{2,1,0:T(8,128)S(1)}, u32[]{:S(2)}, u32[]{:S(2)}) async-start(f32[4,8,128]{2,1,0:T(8,128)} %multiply_bitcast_fusion), calls=%async_computation.2 | async-start | bytes 32768 | tf_op jit(solution)/shard_map/all_to_all | solution.py:29
where the time goes:
time: 80.1 us; the launch traced here: 79.5 us
  blocking collectives  38.5 us (48%)
  starting transfers between devices  14.3 us (18%)
  waiting for transfers between devices  9.37 us (12%)
  matrix products  8.4 us (10%)
  other arithmetic  5.37 us (7%)
  between operations  2.73 us (3%)
  local copies, waits for them, and re-layouts  0.86 us (1%)
    psum x1, blocking collectives, local(): lax.psum((local_coef, jnp.sum(applied * applied), gram_local), ('grp', 'm...  38.5 us
    all_to_all x1, starting transfers between devices, local(): lax.all_to_all(leaf_fiber.astype(jnp.float32), 'mem', split_axis=0, conca...  5.2 us
    all_to_all x1, starting transfers between devices, local(): lax.all_to_all(outgoing, 'grp', split_axis=0, concat_axis=0, tiled=True)  4.88 us
    all_to_all x1, waiting for transfers between devices, local(): lax.all_to_all(outgoing, 'grp', split_axis=0, concat_axis=0, tiled=True)  4.71 us
    all_to_all x1, waiting for transfers between devices, local(): lax.all_to_all(leaf_rows, 'mem', split_axis=0, concat_axis=0, tiled=True)  4.65 us
    all_to_all x1, starting transfers between devices, local(): lax.all_to_all(leaf_rows, 'mem', split_axis=0, concat_axis=0, tiled=True)  4.21 us
    dot_general x1, matrix products, local(): jnp.einsum('kfi,lfi->kl', basis, basis, precision=lax.Precision.HIGHEST)  2.75 us
  transfers between devices with their start and end apart: 3, of which 2 were waited for; matrix products, arithmetic and copies ran while one was open for 7% of the time, Pallas kernels for 0%

commit v1 on v0

--- a/solution.py
+++ b/solution.py
@@ -36,8 +36,9 @@
     total = float(fibers_here * width * groups * members)
     local_coef = jnp.einsum("kfi,fi->k", basis, applied, precision=lax.Precision.HIGHEST)
     gram_local = jnp.einsum("kfi,lfi->kl", basis, basis, precision=lax.Precision.HIGHEST)
-    coef_sum, square_sum, gram_sum = lax.psum(
-        (local_coef, jnp.sum(applied * applied), gram_local), ("grp", "mem")
+    coef_sum, square_sum, gram_sum = jax.lax.psum(
+        jax.lax.psum((local_coef, jnp.sum(applied * applied), gram_local), axis_name="mem"),
+        axis_name="grp",
     )
     coef = coef_sum / total
     gram = gram_sum / total

time: 80.1 us -> 82.1 us (1.025)
  blocking collectives: 38.5 us -> 40.5 us
    psum x1 -> x2, blocking collectives: 38.5 us -> 40.5 us  [the longest x1 23.4 us: local(): jax.lax.psum((local_coef, jnp.sum(applied * applied), gram_local), axis_n...]
where the time goes in v1:
time: 82.1 us; the launch traced here: 81.5 us
  blocking collectives  40.5 us (49%)
  starting transfers between devices  14.3 us (17%)
  waiting for transfers between devices  9.37 us (11%)
  matrix products  8.4 us (10%)
  other arithmetic  5.37 us (7%)
  between operations  2.73 us (3%)
  local copies, waits for them, and re-layouts  0.86 us (1%)
    psum x1, blocking collectives, local(): jax.lax.psum((local_coef, jnp.sum(applied * applied), gram_local), axis_n...  23.4 us
    psum x1, blocking collectives, local(): jax.lax.psum(jax.lax.psum((local_coef, jnp.sum(applied * applied), gram_l...  17.1 us
    all_to_all x1, starting transfers between devices, local(): lax.all_to_all(leaf_fiber.astype(jnp.float32), 'mem', split_axis=0, conca...  5.2 us
    all_to_all x1, starting transfers between devices, local(): lax.all_to_all(outgoing, 'grp', split_axis=0, concat_axis=0, tiled=True)  4.88 us
    all_to_all x1, waiting for transfers between devices, local(): lax.all_to_all(outgoing, 'grp', split_axis=0, concat_axis=0, tiled=True)  4.71 us
    all_to_all x1, waiting for transfers between devices, local(): lax.all_to_all(leaf_rows, 'mem', split_axis=0, concat_axis=0, tiled=True)  4.65 us
    all_to_all x1, starting transfers between devices, local(): lax.all_to_all(leaf_rows, 'mem', split_axis=0, concat_axis=0, tiled=True)  4.21 us
    dot_general x1, matrix products, local(): jnp.einsum('kfi,lfi->kl', basis, basis, precision=lax.Precision.HIGHEST)  2.75 us
  transfers between devices with their start and end apart: 3, of which 2 were waited for; matrix products, arithmetic and copies ran while one was open for 7% of the time, Pallas kernels for 0%

profile of v1, /device:TPU:0, one launch (start us, length us, event | category | flops | bytes accessed | tf_op | source)
XLA Modules:
  0.0 81.5 jit_solution(5662910104804222517)
XLA Ops:
  0.6 0.0 copy-start
  0.6 0.0 copy-start.1
  0.7 0.8 convert_element_type.29
  1.5 0.7 all_to_all.22
  2.1 5.2 %all-to-all-start = ((f32[8,4,1]{1,2,0:T(1,128)}), f32[8,4,1]{1,2,0:T(1,128)S(1)}, u32[]{:S(2)}, u32[]{:S(2)}) async-start(f32[8,4,1]{1,2,0:T(1,128)} %bitcast.1), calls=%async_computation | async-start | bytes 8192 | tf_op jit(solution)/shard_map/all_to_all | solution.py:16
  7.3 0.7 fusion.16
  8.1 0.1 reshape.35
  8.2 1.4 %multiply_bitcast_fusion = f32[4,8,128]{2,1,0:T(8,128)} fusion(f32[32,128]{1,0:T(8,128)} %param.11, f32[32]{0:T(128)S(1)} %reshape.35), kind=kLoop, calls=%fused_computation.21 | loop fusion | flops 4096 | bytes 32896 | tf_op jit(solution)/shard_map/all_to_all | solution.py:29
  9.5 2.8 %convolution_bitcast_fusion = f32[20,20]{1,0:T(8,128)S(1)} fusion(f32[20,64,128]{2,1,0:T(8,128)} %param.7), kind=kOutput, calls=%fused_computation.4 | convolution fusion | flops 39321600 | bytes 656960 | tf_op jit(solution)/shard_map/kfi,lfi->kl/dot_general | solution.py:38
  12.3 0.0 all-to-all-done
  12.3 4.2 %all-to-all-start.1 = ((f32[8,4,128]{2,1,0:T(4,128)}), f32[8,4,128]{2,1,0:T(4,128)S(1)}, u32[]{:S(2)}, u32[]{:S(2)}) async-start(f32[8,4,128]{2,1,0:T(4,128)} %bitcast.45), calls=%async_computation.1 | async-start | bytes 32768 | tf_op jit(solution)/shard_map/all_to_all | solution.py:15
  16.5 0.1 convert_element_type.31
  16.6 4.7 %all-to-all-done.1 = f32[8,4,128]{2,1,0:T(4,128)S(1)} async-done(((f32[8,4,128]{2,1,0:T(4,128)}), f32[8,4,128]{2,1,0:T(4,128)S(1)}, u32[]{:S(2)}, u32[]{:S(2)}) %all-to-all-start.1) | async-done | bytes 16416 | tf_op jit(solution)/shard_map/all_to_all | solution.py:15
  21.3 4.9 %all-to-all-start.2 = ((f32[4,8,128]{2,1,0:T(8,128)}), f32[4,8,128]{2,1,0:T(8,128)S(1)}, u32[]{:S(2)}, u32[]{:S(2)}) async-start(f32[4,8,128]{2,1,0:T(8,128)} %multiply_bitcast_fusion), calls=%async_computation.2 | async-start | bytes 32768 | tf_op jit(solution)/shard_map/all_to_all | solution.py:29
  26.2 0.9 %convolution_add_fusion.1 = f32[64,128]{1,0:T(8,128)S(1)} fusion(f32[32,128]{1,0:T(8,128)S(1)} %bitcast.44, f32[20,64,128]{2,1,0:T(8,128)} %param.7, s32[32]{0:T(128)S(1)} %convert_element_type.31), kind=kOutput, calls=%fused_computation.1 | convolution fusion | flops 3155968 | bytes 82048 | tf_op jit(solution)/shard_map/dot_general | solution.py:21
  27.1 4.7 %all-to-all-done.2 = f32[4,8,128]{2,1,0:T(8,128)S(1)} async-done(((f32[4,8,128]{2,1,0:T(8,128)}), f32[4,8,128]{2,1,0:T(8,128)S(1)}, u32[]{:S(2)}, u32[]{:S(2)}) %all-to-all-start.2) | async-done | bytes 16416 | tf_op jit(solution)/shard_map/all_to_all | solution.py:29
  31.8 0.8 fusion.1
  32.6 0.0 copy-done
  32.6 1.2 %fusion.9 = f32[64,1,128]{2,1,0:T(1,128)S(1)} fusion(bf16[64,128,128]{2,1,0:T(8,128)(2,1)S(1)} %copy-done, bf16[64,128,1]{1,0,2:T(8,128)(2,1)S(1)} %fusion.1), kind=kOutput, calls=%fused_computation.14 | convolution fusion | flops 2097152 | bytes 2146304 | tf_op jit(solution)/shard_map/fij,fj->fi/dot_general | solution.py:35
  33.8 0.0 copy-done.1
  33.8 1.1 %convolution_bitcast_fusion.2 = f32[20]{0:T(128)S(1)} fusion(f32[20,64,128]{2,1,0:T(8,128)S(1)} %copy-done.1, f32[64,1,128]{2,1,0:T(1,128)S(1)} %fusion.9), kind=kOutput, calls=%fused_computation.7 | convolution fusion | flops 1966080 | bytes 688208 | tf_op jit(solution)/shard_map/kfi,fi->k/dot_general | solution.py:37
  34.8 0.6 multiply_reduce_fusion
  35.5 23.4 %all-reduce = (f32[]{:T(128)}, f32[20]{0:T(128)S(1)}, f32[20,20]{1,0:T(8,128)S(1)}) all-reduce(f32[]{:T(128)} %multiply_reduce_fusion, f32[20]{0:T(128)S(1)} %convolution_bitcast_fusion.2, f32[20,20]{1,0:T(8,128)S(1)} %convolution_bitcast_fusion), channel_id=1, replica_groups=mesh['grp'=4,'mem'=8] {'mem'}, use_global_device_ids=true, to_apply=%region_3.0 | all-reduce | flops 421 | bytes 3368 | tf_op jit(solution)/shard_map/psum | solution.py:40
  58.8 17.1 %all-reduce.1 = (f32[]{:T(128)}, f32[20]{0:T(128)S(1)}, f32[20,20]{1,0:T(8,128)S(1)}) all-reduce(f32[]{:T(128)} %get-tuple-element.2, f32[20]{0:T(128)S(1)} %get-tuple-element.3, f32[20,20]{1,0:T(8,128)S(1)} %get-tuple-element.4), channel_id=1, replica_groups=mesh['grp'=4,'mem'=8] {'grp'}, use_global_device_ids=true, to_apply=%region_4.0 | all-reduce | flops 421 | bytes 3368 | tf_op jit(solution)/shard_map/psum | solution.py:39
  76.0 0.6 broadcast_multiply_fusion
  76.6 0.9 %fusion.3 = f32[1,64,128]{2,0,1:T(1,128)S(1)} fusion(f32[20,64,128]{2,1,0:T(8,128)S(1)} %copy-done.1, f32[20]{0:T(128)S(1)} %get-tuple-element.6), kind=kOutput, calls=%fused_computation.8 | convolution fusion | flops 1966100 | bytes 688208 | tf_op jit(solution)/shard_map/k,kfi->fi/dot_general | solution.py:45
  77.5 0.8 %fusion.7 = f32[]{:T(128)} fusion(f32[20,20]{1,0:T(8,128)S(1)} %get-tuple-element.7, f32[20]{0:T(128)S(1)} %get-tuple-element.6), kind=kOutput, calls=%fused_computation.12 | convolution fusion | flops 5279 | bytes 1684 | tf_op jit(solution)/shard_map/dot_general | solution.py:46
  80.3 0.6 subtract_divide_fusion
  80.9 0.6 pad_maximum_fusion
  (1 shorter events, 0.0 us)
Async XLA Ops:
  0.6 31.9 %copy-start = (bf16[64,128,128]{2,1,0:T(8,128)(2,1)S(1)}, bf16[64,128,128]{2,1,0:T(8,128)(2,1)}, u32[]{:S(2)}) copy-start(bf16[64,128,128]{2,1,0:T(8,128)(2,1)} %param.8) | copy-start | bytes 6291460
  0.6 33.1 %copy-start.1 = (f32[20,64,128]{2,1,0:T(8,128)S(1)}, f32[20,64,128]{2,1,0:T(8,128)}, u32[]{:S(2)}) copy-start(f32[20,64,128]{2,1,0:T(8,128)} %param.7) | copy-start | bytes 1966084
  2.1 10.2 %all-to-all-start = ((f32[8,4,1]{1,2,0:T(1,128)}), f32[8,4,1]{1,2,0:T(1,128)S(1)}, u32[]{:S(2)}, u32[]{:S(2)}) async-start(f32[8,4,1]{1,2,0:T(1,128)} %bitcast.1), calls=%async_computation | async-start | bytes 8192 | tf_op jit(solution)/shard_map/all_to_all | solution.py:16
  12.3 9.0 %all-to-all-start.1 = ((f32[8,4,128]{2,1,0:T(4,128)}), f32[8,4,128]{2,1,0:T(4,128)S(1)}, u32[]{:S(2)}, u32[]{:S(2)}) async-start(f32[8,4,128]{2,1,0:T(4,128)} %bitcast.45), calls=%async_computation.1 | async-start | bytes 32768 | tf_op jit(solution)/shard_map/all_to_all | solution.py:15
  21.3 10.5 %all-to-all-start.2 = ((f32[4,8,128]{2,1,0:T(8,128)}), f32[4,8,128]{2,1,0:T(8,128)S(1)}, u32[]{:S(2)}, u32[]{:S(2)}) async-start(f32[4,8,128]{2,1,0:T(8,128)} %multiply_bitcast_fusion), calls=%async_computation.2 | async-start | bytes 32768 | tf_op jit(solution)/shard_map/all_to_all | solution.py:29
